TPU v7x, 32 devices: a whole 2x2x4 slice. The times are simulated.
32 devices in a mesh: groups: 2 (over y), img: 8 (over z, x), sub: 2 (over core).
Axes of the slice: x: 2, y: 2, z: 4, core: 2. Of those that a mesh axis runs over, the one named last changes fastest.
Arguments:
- feats: bfloat16 [16, 128, 256], P(('groups', 'img')), parts along dimension 0
- grad_msg: bfloat16 [16, 128, 256], P(('groups', 'img'), None, 'sub'), parts along dimension 0, may hold values from -6 to 6
- w_qk: bfloat16 [256, 256], P(None, 'sub'), may hold values from -0.375 to 0.375
- w_v: bfloat16 [256, 256], P(None, 'sub'), may hold values from -0.375 to 0.375
- pair_slots: int32 [16, 4, 2], P(('groups', 'img')), parts along dimension 0, may hold values from -1 to 7, as said below
- counts: int32 [16], P(('groups', 'img')), parts along dimension 0, may hold values from 32 to 128, as said below
Outputs:
- grad_feats: bfloat16 [16, 128, 256], P(('groups', 'img'), None, 'sub'), parts along dimension 0
- grad_weights: float32 [4, 256, 256], P('groups', 'img', 'sub'), parts along dimension 0
There are 2 independent parts, one for each index of `groups`. A program takes and returns all parts, laid end to end along the dimension named above; an argument that names none is the same for every part. Nothing has to cross between parts.
Inputs may be any that keep to these rules, and one draw needn't show every extreme that they name: `pair_slots`: row o lists the pairs owned by index o of img: (i, j) with i != j first, its remaining slots -1; 9 pairs in all; some owner lists exactly 4 pairs. `counts`: some image has all 128 keypoints.
All inputs are finite; a program needn't handle non-finite values.
Results may differ from a plain program's by a relative error of at most 0.012.
Values may be sent and summed in bfloat16 or wider, within the bound.
A program may use at most 64 MiB of HBM per device.

v0:
```python
import jax
import jax.numpy as jnp
from jax import lax
from jax.sharding import PartitionSpec as P

HEAD_DIM = 64


NEG_FILL = -1e30


def contract(left, right, left_dim, right_dim):
    return lax.dot_general(
        left, right, (((left_dim,), (right_dim,)), ((), ())), preferred_element_type=jnp.float32
    )


def normalize(scores, axis):
    top = jnp.max(scores, axis=axis, keepdims=True)
    weights = jnp.exp(scores - top)
    return weights / jnp.sum(weights, axis=axis, keepdims=True)


def head_backward(parts, scale):
    q_left, v_left, g_left, q_right, v_right, g_right, m_left, m_right = parts
    scores = contract(q_left, q_right, 1, 1) * scale
    row_probs = normalize(jnp.where(m_right[None, :] > 0, scores, NEG_FILL), 1)
    col_probs = normalize(jnp.where(m_left[:, None] > 0, scores, NEG_FILL), 0)
    gm_left = g_left * m_left[:, None]
    gm_right = g_right * m_right[:, None]
    row_low = row_probs.astype(jnp.bfloat16)
    col_low = col_probs.astype(jnp.bfloat16)
    dv_right = contract(row_low, gm_left, 0, 0)
    dv_left = contract(col_low, gm_right, 1, 0)
    drow = contract(gm_left, v_right, 1, 1)
    dcol = contract(v_left, gm_right, 1, 1)
    dscore = row_probs * (drow - jnp.sum(drow * row_probs, axis=1, keepdims=True))
    dscore = dscore + col_probs * (dcol - jnp.sum(dcol * col_probs, axis=0, keepdims=True))
    dscore_low = (dscore * scale).astype(jnp.bfloat16)
    dq_left = contract(dscore_low, q_right, 1, 0)
    dq_right = contract(dscore_low, q_left, 0, 0)
    return (dq_left, dv_left, dq_right, dv_right)


def slot_backward(block, mask):
    width = block.shape[-1] // 3
    local_heads = width // HEAD_DIM
    rows = block.shape[1]

    def heads_first(part):
        return part.reshape(rows, local_heads, HEAD_DIM).transpose(1, 0, 2)

    pieces = tuple(
        (
            heads_first(block[side, :, kind * width : (kind + 1) * width])
            for side in range(2)
            for kind in range(3)
        )
    )

    def one_head(item):
        return head_backward(item + (mask[0], mask[1]), HEAD_DIM ** (-0.5))

    dq_left, dv_left, dq_right, dv_right = lax.map(one_head, pieces)

    def heads_last(part):
        return part.transpose(1, 0, 2).reshape(rows, width)

    left = jnp.concatenate([heads_last(dq_left), heads_last(dv_left)], axis=1)
    right = jnp.concatenate([heads_last(dq_right), heads_last(dv_right)], axis=1)
    return jnp.stack([left, right]).astype(jnp.bfloat16)


def pair_work(received):
    data, masks = received

    def one_slot(item):
        return slot_backward(item[0], item[1])

    grads = lax.map(one_slot, (data[0], masks[0]))
    count = grads.shape[0]
    rows = grads.shape[2]
    width = grads.shape[3]
    devices = lax.axis_size("img")
    outgoing = grads.reshape(1, count, 2, devices, rows // devices, width)
    return lax.all_to_all(outgoing, "img", split_axis=3, concat_axis=0, tiled=True)


def local(feats, grad_msg, w_qk, w_v, pair_slots, counts):
    devices = lax.axis_size("img")
    here = lax.axis_index("img")
    image = feats[0]
    rows = image.shape[0]
    block_rows = rows // devices
    width = w_qk.shape[1]
    query_keys = jnp.dot(image, w_qk, preferred_element_type=jnp.float32).astype(jnp.bfloat16)
    values = jnp.dot(image, w_v, preferred_element_type=jnp.float32).astype(jnp.bfloat16)
    packed = jnp.concatenate([query_keys, values, grad_msg[0]], axis=1)[None]
    blocks = lax.all_to_all(packed, "img", split_axis=1, concat_axis=0, tiled=True)
    lists, sizes = (
        lax.all_gather(pair_slots, "img", axis=0, tiled=True),
        lax.all_gather(counts, "img", axis=0, tiled=True),
    )
    valid = lists[:, :, 0] >= 0
    ids = jnp.maximum(lists, 0)
    outgoing = blocks[ids]
    row_ids = here * block_rows + jnp.arange(block_rows, dtype=jnp.int32)
    live_rows = valid[:, :, None, None] & (row_ids[None, None, None, :] < sizes[ids][:, :, :, None])
    row_mask = live_rows.astype(jnp.bfloat16)
    returned = pair_work(
        (
            lax.all_to_all(outgoing, "img", split_axis=0, concat_axis=3, tiled=True),
            lax.all_to_all(row_mask, "img", split_axis=0, concat_axis=3, tiled=True),
        )
    )
    slot_count = returned.shape[1]
    flat_grads = returned.reshape(devices * slot_count * 2, block_rows * 2 * width)
    owned = jnp.broadcast_to(valid[:, :, None], ids.shape).reshape(-1)
    onehot = (
        (ids.reshape(-1)[:, None] == jnp.arange(devices, dtype=jnp.int32)[None, :]) & owned[:, None]
    ).astype(jnp.bfloat16)
    totals = contract(onehot, flat_grads, 0, 0).reshape(devices, block_rows, 2 * width)
    summed = lax.all_to_all(
        totals.astype(jnp.bfloat16), "img", split_axis=0, concat_axis=1, tiled=True
    ).astype(totals.dtype)[0]
    grad_qk = summed[:, :width].astype(jnp.bfloat16)
    grad_v = summed[:, width:].astype(jnp.bfloat16)
    both = jnp.concatenate([grad_qk, grad_v], axis=1)
    shares = lax.psum_scatter(contract(image, both, 0, 0), "img", scatter_dimension=0, tiled=True)
    grad_weights = shares.reshape(-1, 2, width).transpose(1, 0, 2)
    term = contract(grad_qk, w_qk, 1, 1) + contract(grad_v, w_v, 1, 1)
    grad_feats = lax.psum_scatter(term, "sub", scatter_dimension=1, tiled=True).astype(jnp.bfloat16)
    return (grad_feats[None], grad_weights)


def solution(mesh):
    in_specs = (
        P(("groups", "img"), None, None),
        P(("groups", "img"), None, "sub"),
        P(None, "sub"),
        P(None, "sub"),
        P(("groups", "img"), None, None),
        P(("groups", "img")),
    )
    out_specs = (P(("groups", "img"), None, "sub"), P("groups", "img", "sub"))
    return jax.shard_map(local, mesh=mesh, in_specs=in_specs, out_specs=out_specs, check_vma=False)
```

profile of v0, /device:TPU:0, one launch (start us, length us, event | category | flops | bytes accessed | tf_op | source)
XLA Modules:
  0.0 209.5 jit_solution(14507012601487618797)
XLA Ops:
  7.2 0.9 copy.113
  9.9 1.2 reduce
  11.8 7.3 %all-to-all-start = ((bf16[8,2,3072]{2,1,0:T(2,128)(2,1)}), bf16[8,2,3072]{2,1,0:T(2,128)(2,1)S(1)}, u32[]{:S(2)}, u32[]{:S(2)}) async-start(bf16[8,2,3072]{2,1,0:T(2,128)(2,1)} %reshape.153), calls=%async_computation | async-start | bytes 196608 | tf_op jit(solution)/shard_map/all_to_all | solution.py:99
  19.7 21.0 %all_gather.6 = s32[8,4,2]{1,2,0:T(2,128)S(1)} all-gather(s32[1,4,2]{1,2,0:T(2,128)S(1)} %copy-done.3), channel_id=1, replica_groups=mesh['groups'=2,'img'=8,'sub'=2] {'img'}, dimensions={0}, use_global_device_ids=true | all-gather | bytes 288 | tf_op jit(solution)/shard_map/all_gather | solution.py:101
  43.7 6.8 %all-reduce = s32[8]{0:T(128)S(1)} all-reduce(s32[8]{0:T(128)S(1)} %dynamic-update-slice), channel_id=1, replica_groups=mesh['groups'=2,'img'=8,'sub'=2] {'img'}, use_global_device_ids=true, to_apply=%add | all-reduce | flops 8 | bytes 64
  52.2 6.3 %all-to-all-start.2 = ((bf16[8,4,2,16]{3,2,1,0:T(2,128)(2,1)}), bf16[8,4,2,16]{3,2,1,0:T(2,128)(2,1)S(1)}, u32[]{:S(2)}, u32[]{:S(2)}) async-start(bf16[8,4,2,16]{3,2,1,0:T(2,128)(2,1)} %and_convert_fusion), calls=%async_computation.2 | async-start | bytes 32768 | tf_op jit(solution)/shard_map/all_to_all | solution.py:113
  58.6 1.5 gather_fusion
  60.2 5.0 %all-to-all-done.2 = bf16[8,4,2,16]{3,2,1,0:T(2,128)(2,1)S(1)} async-done(((bf16[8,4,2,16]{3,2,1,0:T(2,128)(2,1)}), bf16[8,4,2,16]{3,2,1,0:T(2,128)(2,1)S(1)}, u32[]{:S(2)}, u32[]{:S(2)}) %all-to-all-start.2) | async-done | bytes 2080 | tf_op jit(solution)/shard_map/all_to_all | solution.py:113
  65.2 3.5 %all-to-all-start.1 = ((bf16[8,4,2,16,384]{4,3,2,1,0:T(8,128)(2,1)}), bf16[8,4,2,16,384]{4,3,2,1,0:T(8,128)(2,1)S(1)}, u32[]{:S(2)}, u32[]{:S(2)}) async-start(bf16[8,4,2,16,384]{4,3,2,1,0:T(8,128)(2,1)} %bitcast.44), calls=%async_computation.1 | async-start | bytes 1572864 | tf_op jit(solution)/shard_map/all_to_all | solution.py:112
  68.9 13.0 %all-to-all-done.1 = bf16[8,4,2,16,384]{4,3,2,1,0:T(8,128)(2,1)S(1)} async-done(((bf16[8,4,2,16,384]{4,3,2,1,0:T(8,128)(2,1)}), bf16[8,4,2,16,384]{4,3,2,1,0:T(8,128)(2,1)S(1)}, u32[]{:S(2)}, u32[]{:S(2)}) %all-to-all-start.1) | async-done | bytes 786464 | tf_op jit(solution)/shard_map/all_to_all | solution.py:112
  82.0 20.7 %while.27 = (s32[]{:T(128)}, bf16[4,2,128,256]{3,2,1,0:T(8,128)(2,1)S(1)}, bf16[4,2,128,384]{3,2,1,0:T(8,128)(2,1)S(1)}, bf16[4,2,128]{2,1,0:T(2,128)(2,1)S(1)}, s32[]{:T(128)}, /*index=5*/s32[]{:T(128)}, s32[]{:T(128)}) while((s32[]{:T(128)}, bf16[4,2,128,256]{3,2,1,0:T(8,128)(2,1)S(1)}, bf16[4,2,128,384]{3,2,1,0:T(8,128)(2,1)S(1)}, ...), condition=%wide.region_9.10_spmd, body=%wide.region_0.9_spmd.sunk | while | flops 15728132 | bytes 3562074 | solution.py:80
  82.3 4.7 %while.28 = (s32[]{:T(128)}, bf16[2,128,64]{1,2,0:T(8,128)(2,1)S(1)}, bf16[2,128,64]{1,2,0:T(8,128)(2,1)S(1)}, bf16[2,128,64]{1,2,0:T(8,128)(2,1)S(1)}, bf16[2,1...) while((s32[]{:T(128)}, ...), condition=%wide.region_8.8_spmd, body=%wide.region_1.7_spmd.sunk | while | flops 15400450 | bytes 1332625 | solution.py:64
  87.5 4.7 %while.28 = (s32[]{:T(128)}, bf16[2,128,64]{1,2,0:T(8,128)(2,1)S(1)}, bf16[2,128,64]{1,2,0:T(8,128)(2,1)S(1)}, bf16[2,128,64]{1,2,0:T(8,128)(2,1)S(1)}, bf16[2,1...) while((s32[]{:T(128)}, ...), condition=%wide.region_8.8_spmd, body=%wide.region_1.7_spmd.sunk | while | flops 15400450 | bytes 1332625 | solution.py:64
  92.6 4.7 %while.28 = (s32[]{:T(128)}, bf16[2,128,64]{1,2,0:T(8,128)(2,1)S(1)}, bf16[2,128,64]{1,2,0:T(8,128)(2,1)S(1)}, bf16[2,128,64]{1,2,0:T(8,128)(2,1)S(1)}, bf16[2,1...) while((s32[]{:T(128)}, ...), condition=%wide.region_8.8_spmd, body=%wide.region_1.7_spmd.sunk | while | flops 15400450 | bytes 1332625 | solution.py:64
  97.8 4.7 %while.28 = (s32[]{:T(128)}, bf16[2,128,64]{1,2,0:T(8,128)(2,1)S(1)}, bf16[2,128,64]{1,2,0:T(8,128)(2,1)S(1)}, bf16[2,128,64]{1,2,0:T(8,128)(2,1)S(1)}, bf16[2,1...) while((s32[]{:T(128)}, ...), condition=%wide.region_8.8_spmd, body=%wide.region_1.7_spmd.sunk | while | flops 15400450 | bytes 1332625 | solution.py:64
  102.7 0.9 copy.120
  103.5 3.5 %all-to-all-start.3 = ((bf16[1,4,2,8,16,256]{5,4,2,1,0,3:T(8,128)(2,1)}), bf16[1,4,2,8,16,256]{5,4,2,1,0,3:T(8,128)(2,1)S(1)}, u32[]{:S(2)}, u32[]{:S(2)}) async-start(bf16[1,4,2,8,16,256]{5,4,2,1,0,3:T(8,128)(2,1)} %copy.120), calls=%async_computation.3 | async-start | bytes 1048576 | tf_op jit(solution)/shard_map/all_to_all | solution.py:86
  107.3 10.7 %all-to-all-done.3 = bf16[1,4,2,8,16,256]{5,4,2,1,0,3:T(8,128)(2,1)S(1)} async-done(((bf16[1,4,2,8,16,256]{5,4,2,1,0,3:T(8,128)(2,1)}), bf16[1,4,2,8,16,256]{5,4,2,1,0,3:T(8,128)(2,1)S(1)}, u32[]{:S(2)}, u32[]{:S(2)}) %all-to-all-start.3) | async-done | bytes 524320 | tf_op jit(solution)/shard_map/all_to_all | solution.py:86
  118.3 10.3 %all_to_all.66 = bf16[8,16,256]{2,1,0:T(8,128)(2,1)S(1)} all-to-all(bf16[8,16,256]{2,1,0:T(8,128)(2,1)S(1)} %copy.122), channel_id=1, replica_groups=mesh['groups'=2,'img'=8,'sub'=2] {'img'}, dimensions={0} | all-to-all | bytes 131072 | tf_op jit(solution)/shard_map/all_to_all | solution.py:123
  128.8 0.8 convolution_add_fusion
  130.8 4.1 %reduce-scatter.5.cloned.1.call-done = f32[128,128]{1,0:T(8,128)} async-done(((f32[128,256]{1,0:T(8,128)}), f32[128,128]{1,0:T(8,128)}) %reduce-scatter.5.cloned.1.call-update) | async-done | bytes 65552 | tf_op jit(solution)/shard_map/reduce_scatter | solution.py:132
  134.9 1.5 convert_bitcast_fusion
  136.3 64.7 %reduce-scatter.7.cloned.1.call-done = f32[32,256]{1,0:T(8,128)} async-done(((f32[256,256]{1,0:T(8,128)}), f32[32,256]{1,0:T(8,128)}) %reduce-scatter.7.cloned.1.call-update) | async-done | bytes 32784
  201.1 0.9 copy.126
  (217 shorter events, 29.6 us)
Async XLA Ops:
  7.2 0.9 copy-start
  7.2 0.9 copy-start.2
  8.1 0.8 copy-start.1
  11.8 40.4 %all-to-all-start = ((bf16[8,2,3072]{2,1,0:T(2,128)(2,1)}), bf16[8,2,3072]{2,1,0:T(2,128)(2,1)S(1)}, u32[]{:S(2)}, u32[]{:S(2)}) async-start(bf16[8,2,3072]{2,1,0:T(2,128)(2,1)} %reshape.153), calls=%async_computation | async-start | bytes 196608 | tf_op jit(solution)/shard_map/all_to_all | solution.py:99
  19.0 0.7 copy-start.3
  41.6 0.7 copy-start.4
  52.2 13.0 %all-to-all-start.2 = ((bf16[8,4,2,16]{3,2,1,0:T(2,128)(2,1)}), bf16[8,4,2,16]{3,2,1,0:T(2,128)(2,1)S(1)}, u32[]{:S(2)}, u32[]{:S(2)}) async-start(bf16[8,4,2,16]{3,2,1,0:T(2,128)(2,1)} %and_convert_fusion), calls=%async_computation.2 | async-start | bytes 32768 | tf_op jit(solution)/shard_map/all_to_all | solution.py:113
  65.2 16.7 %all-to-all-start.1 = ((bf16[8,4,2,16,384]{4,3,2,1,0:T(8,128)(2,1)}), bf16[8,4,2,16,384]{4,3,2,1,0:T(8,128)(2,1)S(1)}, u32[]{:S(2)}, u32[]{:S(2)}) async-start(bf16[8,4,2,16,384]{4,3,2,1,0:T(8,128)(2,1)} %bitcast.44), calls=%async_computation.1 | async-start | bytes 1572864 | tf_op jit(solution)/shard_map/all_to_all | solution.py:112
  103.5 14.5 %all-to-all-start.3 = ((bf16[1,4,2,8,16,256]{5,4,2,1,0,3:T(8,128)(2,1)}), bf16[1,4,2,8,16,256]{5,4,2,1,0,3:T(8,128)(2,1)S(1)}, u32[]{:S(2)}, u32[]{:S(2)}) async-start(bf16[1,4,2,8,16,256]{5,4,2,1,0,3:T(8,128)(2,1)} %copy.120), calls=%async_computation.3 | async-start | bytes 1048576 | tf_op jit(solution)/shard_map/all_to_all | solution.py:86
  107.1 27.8 %reduce-scatter.5.cloned.1.call-start = ((), (), s32[]{:S(2)}) async-start(), calls=%async_computation.7 | async-start | bytes 196608 | tf_op jit(solution)/shard_map/reduce_scatter | solution.py:132
  129.7 71.4 %reduce-scatter.7.cloned.1.call-start = ((), (), s32[]{:S(2)}) async-start(), calls=%async_computation.8 | async-start | bytes 294912
Sparse Core Ops, SparseCore 0:
  129.8 5.0 reduce-scatter.4
  138.2 62.8 reduce-scatter.6
where the time goes:
time: 210 us; the launch traced here: 209 us
  waiting for transfers between devices  97.7 us (47%)
  blocking collectives  38.1 us (18%)
  starting transfers between devices  20.7 us (10%)
  local copies, waits for them, and re-layouts  15.4 us (7%)
  matrix products  15.1 us (7%)
  between operations  14.9 us (7%)
  other arithmetic  6.63 us (3%)
    unnamed x3, waiting for transfers between devices  64.8 us
    all_gather x1, blocking collectives, local(): lax.all_gather(pair_slots, 'img', axis=0, tiled=True)  21 us
    dot_general x60, matrix products, contract(): lax.dot_general(left, right, (((left_dim,), (right_dim,)), ((), ())), pre...  14.7 us
    all_to_all x1, waiting for transfers between devices, local(): lax.all_to_all(outgoing, 'img', split_axis=0, concat_axis=3, tiled=True)  13 us
    all_to_all x1, waiting for transfers between devices, pair_work(): lax.all_to_all(outgoing, 'img', split_axis=3, concat_axis=0, tiled=True)  10.7 us
    all_to_all x1, blocking collectives, local(): lax.all_to_all(totals.astype(jnp.bfloat16), 'img', split_axis=0, concat_a...  10.3 us
    all_to_all x1, starting transfers between devices, local(): lax.all_to_all(packed, 'img', split_axis=1, concat_axis=0, tiled=True)  7.25 us
    unnamed x20, local copies, waits for them, and re-layouts  7.12 us
  transfers between devices with their start and end apart: 6, of which 5 were waited for; matrix products, arithmetic and copies ran while one was open for 4% of the time, Pallas kernels for 0%

commit v1 on v0

v1 whole, which is shorter than its diff:
```python
import functools

import jax
import jax.numpy as jnp
from jax import lax
from jax.experimental import pallas as pl
from jax.experimental.pallas import tpu as pltpu
from jax.sharding import PartitionSpec as P

HEAD_DIM = 64
NEG_FILL = -1e30
LANES = 128
MESH = pl.DeviceIdType.MESH
ANY = pl.BlockSpec(memory_space=pl.ANY)
VMEM = pl.BlockSpec(memory_space=pltpu.VMEM)
SMEM = pl.BlockSpec(memory_space=pltpu.SMEM)


def contract(left, right, left_dim, right_dim):
    return lax.dot_general(
        left, right, (((left_dim,), (right_dim,)), ((), ())), preferred_element_type=jnp.float32
    )


def loop(low, high, body):
    if high - low <= 8:
        for d in range(low, high):
            body(d)
    else:

        def step(d, carry):
            body(d)
            return carry

        lax.fori_loop(low, high, step, 0)


def kernel(
    n, feats, grad, w_qk_in, w_v_in, pairs, counts, grad_feats, grad_weights,
    all_feats, all_grad, table, w_qk, w_v, acc, terms, outgoing, arrived, term, term_in,
    local_sem, zf_send, zg_send, xf_send, xg_send, c_send, t_send, f_recv, g_recv, c_recv, t_recv,
    w_send, w_recv, s_send, s_recv,
):
    me = lax.axis_index("img")
    sub = lax.axis_index("sub")
    columns = n // 2
    z, x = me // 2, lax.rem(me, 2)
    rows = feats.shape[1]
    half = rows // 2
    width = w_qk.shape[1]
    heads = width // HEAD_DIM
    scale = HEAD_DIM ** (-0.5)
    share = terms.shape[1]
    mine = pl.ds(pl.multiple_of(sub * half, half), half)
    other = pl.ds(pl.multiple_of((1 - sub) * half, half), half)
    across = {"img": z * 2 + 1 - x}
    partner = {"sub": 1 - sub}

    barrier = pltpu.get_barrier_semaphore()
    loop(1, n, lambda d: pl.semaphore_signal(
        barrier, inc=1, device_id={"img": lax.rem(me + d, n)}, device_id_type=MESH
    ))
    pl.semaphore_signal(barrier, inc=1, device_id=partner, device_id_type=MESH)

    own = [
        pltpu.make_async_copy(feats.at[0], all_feats.at[me], local_sem.at[0]),
        pltpu.make_async_copy(w_qk_in, w_qk, local_sem.at[1]),
        pltpu.make_async_copy(w_v_in, w_v, local_sem.at[2]),
        pltpu.make_async_copy(grad.at[0], all_grad.at[me], local_sem.at[3]),
    ]
    for copy in own:
        copy.start()

    lane = lax.broadcasted_iota(jnp.int32, (1, LANES), 1)
    codes = jnp.full((1, LANES), -1, jnp.int32)
    for k in range(pairs.shape[1]):
        left, right = pairs[0, k, 0], pairs[0, k, 1]
        codes = jnp.where(lane == k, jnp.where(left >= 0, left * n + right, -1), codes)
    table[me] = jnp.concatenate([codes, jnp.full((1, LANES), counts[0], jnp.int32)], axis=0)
    pl.semaphore_wait(barrier, n)

    def push(src, dst, send, recv, device):
        return pltpu.make_async_remote_copy(
            src_ref=src, dst_ref=dst, send_sem=send, recv_sem=recv,
            device_id=device, device_id_type=MESH,
        )

    def column(d):
        return lax.rem(z + columns - d, columns) * 2

    def feats_x(block, d):
        return push(
            all_feats.at[block, mine], all_feats.at[block, mine], xf_send.at[d], f_recv.at[block], across
        )

    def grad_x(block, d):
        return push(all_grad.at[block], all_grad.at[block], xg_send.at[d], g_recv.at[block], across)

    def own_feats(send, device):
        return push(feats.at[0, mine], all_feats.at[me, mine], send, f_recv.at[me], device)

    def own_grad(send, device):
        return push(grad.at[0], all_grad.at[me], send, g_recv.at[me], device)

    def column_target(d):
        return {"img": lax.rem(z + d, columns) * 2 + x}

    def core(block, half_rows):
        return push(
            all_feats.at[block, half_rows], all_feats.at[block, half_rows], c_send.at[block],
            c_recv.at[block], partner,
        )

    def table_copy(d):
        return push(
            table.at[me], table.at[me], t_send.at[d], t_recv.at[me], {"img": lax.rem(me + d, n)}
        )

    def table_wait(d):
        block = lax.rem(me + d, n)
        push(
            table.at[block], table.at[block], t_send.at[d], t_recv.at[block], {"img": block}
        ).wait_recv()

    loop(1, n, lambda d: table_copy(d).start())
    own_feats(xf_send.at[0], across).start()
    own_grad(xg_send.at[0], across).start()

    def send_column(d):
        own_feats(zf_send.at[d], column_target(d)).start()
        own_grad(zg_send.at[d], column_target(d)).start()

    loop(1, columns, send_column)

    def arrive_column(d):
        block = column(d) + x
        feats_x(block, d).wait_recv()
        feats_x(block, d).start()
        core(block, mine).start()
        grad_x(block, d).wait_recv()
        grad_x(block, d).start()

    def arrive_across(d):
        block = column(d) + 1 - x
        feats_x(block, d).wait_recv()
        core(block, mine).start()
        grad_x(block, d).wait_recv()

    for copy in own:
        copy.wait()

    row_ids = lax.broadcasted_iota(jnp.int32, (rows, width), 0)

    def project(which):
        f = all_feats[which]
        q = jnp.dot(f, w_qk[...], preferred_element_type=jnp.float32).astype(jnp.bfloat16)
        v = jnp.dot(f, w_v[...], preferred_element_type=jnp.float32).astype(jnp.bfloat16)
        count = table[which, 1:2, :]
        g = jnp.where(row_ids < count, all_grad[which], jnp.zeros((), jnp.bfloat16))
        return q, v, g, count

    def stack(part):
        head = lax.broadcasted_iota(jnp.int32, part.shape, 1) // HEAD_DIM
        zero = jnp.zeros((), part.dtype)
        return jnp.concatenate([jnp.where(head == h, part, zero) for h in range(heads)], axis=0)

    q_own, v_own, g_own, count_own = project(me)
    wide = (rows, heads * rows)
    row_live = lax.broadcasted_iota(jnp.int32, wide, 0) < jnp.concatenate([count_own] * heads, axis=1)
    acc[...] = jnp.zeros_like(acc)
    loop(1, n, table_wait)

    def work(peer):
        core(peer, other).wait_recv()
        q_peer, v_peer, g_peer, count_peer = project(peer)
        q_peer, v_peer, g_peer = stack(q_peer), stack(v_peer), stack(g_peer)
        listed = table[:, 0, :]
        hits = (listed == me * n + peer) | (listed == peer * n + me)
        times = jnp.sum(hits.astype(jnp.float32), keepdims=True)
        scores = contract(q_own, q_peer, 1, 1) * scale
        drow = contract(g_own, v_peer, 1, 1)
        dcol = contract(v_own, g_peer, 1, 1)
        masked = jnp.where(row_live, scores, NEG_FILL)
        e = jnp.exp(masked - jnp.max(masked, axis=0, keepdims=True))
        col = e * (1.0 / jnp.sum(e, axis=0, keepdims=True))
        dcol = col * (dcol - jnp.sum(dcol * col, axis=0, keepdims=True))
        col_live = lax.broadcasted_iota(jnp.int32, (rows, rows), 1) < count_peer
        pieces = []
        for h in range(heads):
            part = slice(h * rows, (h + 1) * rows)
            masked = jnp.where(col_live, scores[:, part], NEG_FILL)
            e = jnp.exp(masked - jnp.max(masked, axis=1, keepdims=True))
            row = e * (1.0 / jnp.sum(e, axis=1, keepdims=True))
            d = drow[:, part]
            d = row * (d - jnp.sum(d * row, axis=1, keepdims=True))
            pieces.append(((d + dcol[:, part]) * scale).astype(jnp.bfloat16))
        dscore = jnp.concatenate(pieces, axis=1)
        acc[:, :width] += times * contract(dscore, q_peer, 1, 0)
        acc[:, width:] += times * contract(col.astype(jnp.bfloat16), g_peer, 1, 0)

    def next_column(d):
        arrive_column(d)
        work(column(d - 1) + x)

    def next_across(d):
        arrive_across(d)
        work(column(d - 1) + 1 - x)

    arrive_across(0)
    arrive_column(1)
    work(column(0) + 1 - x)
    loop(2, columns, next_column)
    arrive_across(1)
    work(column(columns - 1) + x)
    loop(2, columns, next_across)
    work(column(columns - 1) + 1 - x)

    both = acc[...].astype(jnp.bfloat16)
    products = contract(all_feats[me], both, 0, 0)
    for c in range(n):
        piece = products[c * share : (c + 1) * share]
        terms[c] = piece
        outgoing[c] = piece.astype(jnp.bfloat16)

    def weight_copy(d):
        target = lax.rem(me + d, n)
        return push(
            outgoing.at[target], arrived.at[n - d], w_send.at[d], w_recv.at[n - d], {"img": target}
        )

    loop(1, n, lambda d: weight_copy(d).start())
    for c in range(2):
        part = slice(c * width, (c + 1) * width)
        term[c] = contract(both[:, :width], w_qk[part], 1, 1) + contract(
            both[:, width:], w_v[part], 1, 1
        )
    swap = push(term.at[1 - sub], term_in, s_send.at[0], s_recv.at[0], partner)
    swap.start()
    swap.wait_recv()
    grad_feats[0] = (term[sub] + term_in[...]).astype(grad_feats.dtype)

    total = terms[me]
    loop(1, n, lambda d: weight_copy(d).wait_recv())
    for d in range(1, n):
        total = total + arrived[d].astype(jnp.float32)
    grad_weights[0] = total[:, :width]
    grad_weights[1] = total[:, width:]

    swap.wait_send()
    loop(1, n, lambda d: weight_copy(d).wait_send())
    loop(1, n, lambda d: table_copy(d).wait_send())
    own_feats(xf_send.at[0], across).wait_send()
    own_grad(xg_send.at[0], across).wait_send()

    def sent_column(d):
        own_feats(zf_send.at[d], column_target(d)).wait_send()
        own_grad(zg_send.at[d], column_target(d)).wait_send()
        feats_x(column(d) + x, d).wait_send()
        grad_x(column(d) + x, d).wait_send()

    loop(1, columns, sent_column)
    loop(1, n, lambda d: core(lax.rem(me + d, n), mine).wait_send())


def local(feats, grad_msg, w_qk, w_v, pair_slots, counts):
    n = lax.axis_size("img")
    rows, depth = feats.shape[1:]
    width = w_qk.shape[1]
    share = depth // n
    low, full = jnp.bfloat16, jnp.float32
    vmem = pltpu.VMEM
    dma = pltpu.SemaphoreType.DMA
    return pl.pallas_call(
        functools.partial(kernel, n),
        out_shape=(
            jax.ShapeDtypeStruct((1, rows, width), low),
            jax.ShapeDtypeStruct((2, share, width), full),
        ),
        in_specs=[ANY] * 4 + [SMEM] * 2,
        out_specs=(VMEM,) * 2,
        scratch_shapes=[
            vmem((n, rows, depth), low),
            vmem((n, rows, width), low),
            vmem((n, 2, LANES), jnp.int32),
            vmem((depth, width), low),
            vmem((depth, width), low),
            vmem((rows, 2 * width), full),
            vmem((n, share, 2 * width), full),
            vmem((n, share, 2 * width), low),
            vmem((n, share, 2 * width), low),
            vmem((2, rows, width), full),
            vmem((rows, width), full),
            dma((4,)),
            dma((n // 2,)), dma((n // 2,)), dma((n // 2,)), dma((n // 2,)),
            dma((n,)), dma((n,)), dma((n,)), dma((n,)), dma((n,)), dma((n,)),
            dma((n,)), dma((n,)), dma((1,)), dma((1,)),
        ],
        compiler_params=pltpu.CompilerParams(
            collective_id=0, has_side_effects=True, vmem_limit_bytes=40 * 1024 * 1024
        ),
        name="backward",
    )(feats, grad_msg, w_qk, w_v, pair_slots, counts)


def solution(mesh):
    in_specs = (
        P(("groups", "img"), None, None),
        P(("groups", "img"), None, "sub"),
        P(None, "sub"),
        P(None, "sub"),
        P(("groups", "img"), None, None),
        P(("groups", "img")),
    )
    out_specs = (P(("groups", "img"), None, "sub"), P("groups", "img", "sub"))
    return jax.shard_map(local, mesh=mesh, in_specs=in_specs, out_specs=out_specs, check_vma=False)
```

time: 210 us -> 30.7 us (0.15)
  waiting for transfers between devices: 97.7 us -> 0 us
  blocking collectives: 38.1 us -> 0 us
  Pallas kernels: 0 us -> 24.4 us
  starting transfers between devices: 20.7 us -> 0 us
  matrix products: 15.1 us -> 0 us
  between operations: 14.9 us -> 1.31 us
  local copies, waits for them, and re-layouts: 15.4 us -> 4.61 us
  other arithmetic: 6.63 us -> 0 us
    unnamed x3 -> x0, waiting for transfers between devices: 64.8 us -> none
    all_to_all x4 -> x0, waiting for transfers between devices: 28.8 us -> none  [the longest x1 13 us: local(): lax.all_to_all(outgoing, 'img', split_axis=0, concat_axis=3, tiled=True)]
    pallas_call x0 -> x1, Pallas kernels: none -> 24.4 us  [local(): pl.pallas_call(functools.partial(kernel, n), out_shape=(jax.ShapeDtypeStr...]
    all_gather x1 -> x0, blocking collectives: 21 us -> none  [local(): lax.all_gather(pair_slots, 'img', axis=0, tiled=True)]
    all_to_all x4 -> x0, starting transfers between devices: 20.7 us -> none  [the longest x1 7.25 us: local(): lax.all_to_all(packed, 'img', split_axis=1, concat_axis=0, tiled=True)]
    dot_general x62 -> x0, matrix products: 15.1 us -> none  [the longest x60 14.7 us: contract(): lax.dot_general(left, right, (((left_dim,), (right_dim,)), ((), ())), pre...]
    all_to_all x1 -> x0, blocking collectives: 10.3 us -> none  [local(): lax.all_to_all(totals.astype(jnp.bfloat16), 'img', split_axis=0, concat_a...]
    unnamed x1 -> x0, blocking collectives: 6.79 us -> none
  transfers between devices with their start and end apart: 6 -> 0, of which waited for: 5 -> 0; matrix products, arithmetic and copies ran while one was open for 4% -> 0% of each run, Pallas kernels for 0% -> 0%
where the time goes in v1:
time: 30.7 us; the launch traced here: 30.3 us
  Pallas kernels  24.4 us (79%)
  local copies, waits for them, and re-layouts  4.61 us (15%)
  between operations  1.31 us (4%)
    pallas_call x1, Pallas kernels, local(): pl.pallas_call(functools.partial(kernel, n), out_shape=(jax.ShapeDtypeStr...  24.4 us
    unnamed x13, local copies, waits for them, and re-layouts  4.61 us

profile of v1, /device:TPU:0, one launch (start us, length us, event | category | flops | bytes accessed | tf_op | source)
XLA Modules:
  0.0 30.3 jit_solution(4293526807187654871)
XLA Ops:
  0.6 0.0 copy-start.4
  1.3 0.0 copy-done.4
  1.3 0.1 copy.8.pairs
  1.4 0.0 copy-start
  1.4 0.8 %copy-done = bf16[1,128,256]{2,1,0:T(8,128)(2,1)S(1)} copy-done((bf16[1,128,256]{2,1,0:T(8,128)(2,1)S(1)}, bf16[1,128,256]{2,1,0:T(8,128)(2,1)}, u32[]{:S(2)}) %copy-start) | copy-done | bytes 65560
  2.2 0.0 copy-start.1
  2.2 0.8 %copy-done.1 = bf16[256,128]{1,0:T(8,128)(2,1)S(1)} copy-done((bf16[256,128]{1,0:T(8,128)(2,1)S(1)}, bf16[256,128]{1,0:T(8,128)(2,1)}, u32[]{:S(2)}) %copy-start.1) | copy-done | bytes 65560
  3.1 0.0 copy-start.2
  3.1 0.8 %copy-done.2 = bf16[256,128]{1,0:T(8,128)(2,1)S(1)} copy-done((bf16[256,128]{1,0:T(8,128)(2,1)S(1)}, bf16[256,128]{1,0:T(8,128)(2,1)}, u32[]{:S(2)}) %copy-start.2) | copy-done | bytes 65560
  3.9 0.0 copy-start.3
  3.9 0.8 %copy-done.3 = bf16[1,128,128]{2,1,0:T(8,128)(2,1)S(1)} copy-done((bf16[1,128,128]{2,1,0:T(8,128)(2,1)S(1)}, bf16[1,128,128]{2,1,0:T(8,128)(2,1)}, u32[]{:S(2)}) %copy-start.3) | copy-done | bytes 32792
  4.7 24.4 %backward.1 = (bf16[1,128,128]{2,1,0:T(8,128)(2,1)S(1)}, f32[2,32,128]{2,1,0:T(8,128)S(1)}) custom-call(bf16[1,128,256]{2,1,0:T(8,128)(2,1)S(1)} %copy-done, bf16[1,128,128]{2,1,0:T(8,128)(2,1)S(1)} %copy-done.3, bf16[256,128]{1,0:T(8,128)(2,1)S(1)} %copy-done.1, bf16[256,128]{1,0:T(8,128)(2,1)S(1)} %copy-done.2, s32[1,4,2]{2,1,0:T(4,128)S(1)} %copy.8.pairs, ...), custom_call_target="tpu_custom_call" | custom-call | tf_op jit(solution)/shard_map/backward/pallas_call | solution.py:273
  29.1 0.6 %copy.12 = bf16[1,128,128]{2,1,0:T(8,128)(2,1)} copy(bf16[1,128,128]{2,1,0:T(8,128)(2,1)S(1)} %get-tuple-element.4) | data formatting | bytes 65536
  29.7 0.6 %copy.13 = f32[2,32,128]{2,1,0:T(8,128)} copy(f32[2,32,128]{2,1,0:T(8,128)S(1)} %get-tuple-element.5) | data formatting | bytes 65536
Async XLA Ops:
  0.6 0.7 %copy-start.4 = (s32[1,4,2]{1,2,0:T(2,128)S(1)}, s32[1,4,2]{1,2,0:T(2,128)}, u32[]{:S(2)}) copy-start(s32[1,4,2]{1,2,0:T(2,128)} %param.10) | copy-start | bytes 100
  1.4 0.8 %copy-start = (bf16[1,128,256]{2,1,0:T(8,128)(2,1)S(1)}, bf16[1,128,256]{2,1,0:T(8,128)(2,1)}, u32[]{:S(2)}) copy-start(bf16[1,128,256]{2,1,0:T(8,128)(2,1)} %feats.1) | copy-start | bytes 196612
  2.2 0.8 %copy-start.1 = (bf16[256,128]{1,0:T(8,128)(2,1)S(1)}, bf16[256,128]{1,0:T(8,128)(2,1)}, u32[]{:S(2)}) copy-start(bf16[256,128]{1,0:T(8,128)(2,1)} %w_qk_in.1) | copy-start | bytes 196612
  3.1 0.8 %copy-start.2 = (bf16[256,128]{1,0:T(8,128)(2,1)S(1)}, bf16[256,128]{1,0:T(8,128)(2,1)}, u32[]{:S(2)}) copy-start(bf16[256,128]{1,0:T(8,128)(2,1)} %w_v_in.1) | copy-start | bytes 196612
  3.9 0.8 %copy-start.3 = (bf16[1,128,128]{2,1,0:T(8,128)(2,1)S(1)}, bf16[1,128,128]{2,1,0:T(8,128)(2,1)}, u32[]{:S(2)}) copy-start(bf16[1,128,128]{2,1,0:T(8,128)(2,1)} %grad.1) | copy-start | bytes 98308

commit v2 on v1

--- a/solution.py
+++ b/solution.py
@@ -11,7 +11,7 @@
 NEG_FILL = -1e30
 LANES = 128
 MESH = pl.DeviceIdType.MESH
-ANY = pl.BlockSpec(memory_space=pl.ANY)
+HBM = pl.BlockSpec(memory_space=pltpu.HBM)
 VMEM = pl.BlockSpec(memory_space=pltpu.VMEM)
 SMEM = pl.BlockSpec(memory_space=pltpu.SMEM)
 
@@ -73,8 +73,8 @@
 
     lane = lax.broadcasted_iota(jnp.int32, (1, LANES), 1)
     codes = jnp.full((1, LANES), -1, jnp.int32)
-    for k in range(pairs.shape[1]):
-        left, right = pairs[0, k, 0], pairs[0, k, 1]
+    for k in range(pairs.shape[2]):
+        left, right = pairs[0, 0, k], pairs[0, 1, k]
         codes = jnp.where(lane == k, jnp.where(left >= 0, left * n + right, -1), codes)
     table[me] = jnp.concatenate([codes, jnp.full((1, LANES), counts[0], jnp.int32)], axis=0)
     pl.semaphore_wait(barrier, n)
@@ -86,7 +86,11 @@
         )
 
     def column(d):
-        return lax.rem(z + columns - d, columns) * 2
+        meets, bit = z, 1
+        while bit < columns:
+            meets = meets + (d // bit % 2) * (bit - 2 * bit * (z // bit % 2))
+            bit *= 2
+        return meets * 2
 
     def feats_x(block, d):
         return push(
@@ -103,7 +107,7 @@
         return push(grad.at[0], all_grad.at[me], send, g_recv.at[me], device)
 
     def column_target(d):
-        return {"img": lax.rem(z + d, columns) * 2 + x}
+        return {"img": column(d) + x}
 
     def core(block, half_rows):
         return push(
@@ -130,7 +134,7 @@
         own_feats(zf_send.at[d], column_target(d)).start()
         own_grad(zg_send.at[d], column_target(d)).start()
 
-    loop(1, columns, send_column)
+    loop(1, columns, lambda d: send_column(d))
 
     def arrive_column(d):
         block = column(d) + x
@@ -168,7 +172,6 @@
     wide = (rows, heads * rows)
     row_live = lax.broadcasted_iota(jnp.int32, wide, 0) < jnp.concatenate([count_own] * heads, axis=1)
     acc[...] = jnp.zeros_like(acc)
-    loop(1, n, table_wait)
 
     def work(peer):
         core(peer, other).wait_recv()
@@ -208,6 +211,7 @@
 
     arrive_across(0)
     arrive_column(1)
+    loop(1, n, table_wait)
     work(column(0) + 1 - x)
     loop(2, columns, next_column)
     arrive_across(1)
@@ -276,7 +280,7 @@
             jax.ShapeDtypeStruct((1, rows, width), low),
             jax.ShapeDtypeStruct((2, share, width), full),
         ),
-        in_specs=[ANY] * 4 + [SMEM] * 2,
+        in_specs=[HBM] * 4 + [SMEM] * 2,
         out_specs=(VMEM,) * 2,
         scratch_shapes=[
             vmem((n, rows, depth), low),
@@ -296,10 +300,10 @@
             dma((n,)), dma((n,)), dma((1,)), dma((1,)),
         ],
         compiler_params=pltpu.CompilerParams(
-            collective_id=0, has_side_effects=True, vmem_limit_bytes=40 * 1024 * 1024
+            collective_id=0, has_side_effects=True, vmem_limit_bytes=64 * 1024 * 1024
         ),
         name="backward",
-    )(feats, grad_msg, w_qk, w_v, pair_slots, counts)
+    )(feats, grad_msg, w_qk, w_v, jnp.transpose(pair_slots, (0, 2, 1)), counts)
 
 
 def solution(mesh):

time: 30.7 us -> 28.2 us (0.919)
  local copies, waits for them, and re-layouts: 4.61 us -> 2 us
    unnamed x13 -> x4, local copies, waits for them, and re-layouts: 4.61 us -> 2 us
where the time goes in v2:
time: 28.2 us; the launch traced here: 28 us
  Pallas kernels  24.7 us (88%)
  local copies, waits for them, and re-layouts  2 us (7%)
  between operations  1.29 us (5%)
    pallas_call x1, Pallas kernels, local(): pl.pallas_call(functools.partial(kernel, n), out_shape=(jax.ShapeDtypeStr...  24.7 us
    unnamed x4, local copies, waits for them, and re-layouts  2 us

profile of v2, /device:TPU:0, one launch (start us, length us, event | category | flops | bytes accessed | tf_op | source)
XLA Modules:
  0.0 28.0 jit_solution(16991560618742206213)
XLA Ops:
  1.3 24.7 %backward.1 = (bf16[1,128,128]{2,1,0:T(8,128)(2,1)}, f32[2,32,128]{2,1,0:T(8,128)}) custom-call(bf16[1,128,256]{2,1,0:T(8,128)(2,1)} %feats.1, bf16[1,128,128]{2,1,0:T(8,128)(2,1)} %grad.1, bf16[256,128]{1,0:T(8,128)(2,1)} %w_qk_in.1, bf16[256,128]{1,0:T(8,128)(2,1)} %w_v_in.1, s32[1,2,4]{2,1,0:T(2,128)} %bitcast.1, s32[1]{0:T(128)S(6)} %copy.10.counts), custom_call_target="tpu_custom_call" | custom-call | tf_op jit(solution)/shard_map/backward/pallas_call | solution.py:277
  26.0 0.0 copy-start
  26.0 1.4 %copy.11 = bf16[1,128,128]{2,1,0:T(8,128)(2,1)} copy(bf16[1,128,128]{2,1,0:T(8,128)(2,1)} %get-tuple-element.4) | data formatting | bytes 65536
  27.4 0.0 copy-done
  27.4 0.6 %copy.12 = f32[2,32,128]{2,1,0:T(8,128)} copy(f32[2,32,128]{2,1,0:T(8,128)S(1)} %copy-done) | data formatting | bytes 65536
Async XLA Ops:
  26.0 1.4 %copy-start = (f32[2,32,128]{2,1,0:T(8,128)S(1)}, f32[2,32,128]{2,1,0:T(8,128)}, u32[]{:S(2)}) copy-start(f32[2,32,128]{2,1,0:T(8,128)} %get-tuple-element.5) | copy-start | bytes 98308

commit v3 on v2

--- a/solution.py
+++ b/solution.py
@@ -37,7 +37,7 @@
 
 def kernel(
     n, feats, grad, w_qk_in, w_v_in, pairs, counts, grad_feats, grad_weights,
-    all_feats, all_grad, table, w_qk, w_v, acc, terms, outgoing, arrived, term, term_in,
+    all_feats, all_grad, table, weights, acc, terms, outgoing, arrived, term, term_in,
     local_sem, zf_send, zg_send, xf_send, xg_send, c_send, t_send, f_recv, g_recv, c_recv, t_recv,
     w_send, w_recv, s_send, s_recv,
 ):
@@ -47,7 +47,7 @@
     z, x = me // 2, lax.rem(me, 2)
     rows = feats.shape[1]
     half = rows // 2
-    width = w_qk.shape[1]
+    width = w_qk_in.shape[1]
     heads = width // HEAD_DIM
     scale = HEAD_DIM ** (-0.5)
     share = terms.shape[1]
@@ -64,8 +64,8 @@
 
     own = [
         pltpu.make_async_copy(feats.at[0], all_feats.at[me], local_sem.at[0]),
-        pltpu.make_async_copy(w_qk_in, w_qk, local_sem.at[1]),
-        pltpu.make_async_copy(w_v_in, w_v, local_sem.at[2]),
+        pltpu.make_async_copy(w_qk_in, weights.at[:, pl.ds(0, width)], local_sem.at[1]),
+        pltpu.make_async_copy(w_v_in, weights.at[:, pl.ds(width, width)], local_sem.at[2]),
         pltpu.make_async_copy(grad.at[0], all_grad.at[me], local_sem.at[3]),
     ]
     for copy in own:
@@ -77,6 +77,8 @@
         left, right = pairs[0, 0, k], pairs[0, 1, k]
         codes = jnp.where(lane == k, jnp.where(left >= 0, left * n + right, -1), codes)
     table[me] = jnp.concatenate([codes, jnp.full((1, LANES), counts[0], jnp.int32)], axis=0)
+    for copy in own:
+        copy.wait()
     pl.semaphore_wait(barrier, n)
 
     def push(src, dst, send, recv, device):
@@ -101,10 +103,10 @@
         return push(all_grad.at[block], all_grad.at[block], xg_send.at[d], g_recv.at[block], across)
 
     def own_feats(send, device):
-        return push(feats.at[0, mine], all_feats.at[me, mine], send, f_recv.at[me], device)
+        return push(all_feats.at[me, mine], all_feats.at[me, mine], send, f_recv.at[me], device)
 
     def own_grad(send, device):
-        return push(grad.at[0], all_grad.at[me], send, g_recv.at[me], device)
+        return push(all_grad.at[me], all_grad.at[me], send, g_recv.at[me], device)
 
     def column_target(d):
         return {"img": column(d) + x}
@@ -150,15 +152,11 @@
         core(block, mine).start()
         grad_x(block, d).wait_recv()
 
-    for copy in own:
-        copy.wait()
-
     row_ids = lax.broadcasted_iota(jnp.int32, (rows, width), 0)
 
     def project(which):
-        f = all_feats[which]
-        q = jnp.dot(f, w_qk[...], preferred_element_type=jnp.float32).astype(jnp.bfloat16)
-        v = jnp.dot(f, w_v[...], preferred_element_type=jnp.float32).astype(jnp.bfloat16)
+        projected = contract(all_feats[which], weights[...], 1, 0).astype(jnp.bfloat16)
+        q, v = projected[:, :width], projected[:, width:]
         count = table[which, 1:2, :]
         g = jnp.where(row_ids < count, all_grad[which], jnp.zeros((), jnp.bfloat16))
         return q, v, g, count
@@ -234,12 +232,21 @@
 
     loop(1, n, lambda d: weight_copy(d).start())
     for c in range(2):
-        part = slice(c * width, (c + 1) * width)
-        term[c] = contract(both[:, :width], w_qk[part], 1, 1) + contract(
-            both[:, width:], w_v[part], 1, 1
-        )
+        term[c] = contract(both, weights[c * width : (c + 1) * width], 1, 1)
     swap = push(term.at[1 - sub], term_in, s_send.at[0], s_recv.at[0], partner)
     swap.start()
+    loop(1, n, lambda d: table_copy(d).wait_send())
+    own_feats(xf_send.at[0], across).wait_send()
+    own_grad(xg_send.at[0], across).wait_send()
+
+    def sent_column(d):
+        own_feats(zf_send.at[d], column_target(d)).wait_send()
+        own_grad(zg_send.at[d], column_target(d)).wait_send()
+        feats_x(column(d) + x, d).wait_send()
+        grad_x(column(d) + x, d).wait_send()
+
+    loop(1, columns, sent_column)
+    loop(1, n, lambda d: core(lax.rem(me + d, n), mine).wait_send())
     swap.wait_recv()
     grad_feats[0] = (term[sub] + term_in[...]).astype(grad_feats.dtype)
 
@@ -252,18 +259,6 @@
 
     swap.wait_send()
     loop(1, n, lambda d: weight_copy(d).wait_send())
-    loop(1, n, lambda d: table_copy(d).wait_send())
-    own_feats(xf_send.at[0], across).wait_send()
-    own_grad(xg_send.at[0], across).wait_send()
-
-    def sent_column(d):
-        own_feats(zf_send.at[d], column_target(d)).wait_send()
-        own_grad(zg_send.at[d], column_target(d)).wait_send()
-        feats_x(column(d) + x, d).wait_send()
-        grad_x(column(d) + x, d).wait_send()
-
-    loop(1, columns, sent_column)
-    loop(1, n, lambda d: core(lax.rem(me + d, n), mine).wait_send())
 
 
 def local(feats, grad_msg, w_qk, w_v, pair_slots, counts):
@@ -286,8 +281,7 @@
             vmem((n, rows, depth), low),
             vmem((n, rows, width), low),
             vmem((n, 2, LANES), jnp.int32),
-            vmem((depth, width), low),
-            vmem((depth, width), low),
+            vmem((depth, 2 * width), low),
             vmem((rows, 2 * width), full),
             vmem((n, share, 2 * width), full),
             vmem((n, share, 2 * width), low),

time: 28.2 us -> 28.1 us (level)
  no operation moved by 1% of the time
where the time goes in v3:
time: 28.1 us; the launch traced here: 27.8 us
  Pallas kernels  24.5 us (87%)
  local copies, waits for them, and re-layouts  2 us (7%)
  between operations  1.29 us (5%)
    pallas_call x1, Pallas kernels, local(): pl.pallas_call(functools.partial(kernel, n), out_shape=(jax.ShapeDtypeStr...  24.5 us
    unnamed x4, local copies, waits for them, and re-layouts  2 us

profile of v3, /device:TPU:0, one launch (start us, length us, event | category | flops | bytes accessed | tf_op | source)
XLA Modules:
  0.0 27.8 jit_solution(8107547344663828205)
XLA Ops:
  1.3 24.5 %backward.1 = (bf16[1,128,128]{2,1,0:T(8,128)(2,1)}, f32[2,32,128]{2,1,0:T(8,128)}) custom-call(bf16[1,128,256]{2,1,0:T(8,128)(2,1)} %feats.1, bf16[1,128,128]{2,1,0:T(8,128)(2,1)} %grad.1, bf16[256,128]{1,0:T(8,128)(2,1)} %w_qk_in.1, bf16[256,128]{1,0:T(8,128)(2,1)} %w_v_in.1, s32[1,2,4]{2,1,0:T(2,128)} %bitcast.1, s32[1]{0:T(128)S(6)} %copy.10.counts), custom_call_target="tpu_custom_call" | custom-call | tf_op jit(solution)/shard_map/backward/pallas_call | solution.py:272
  25.8 0.0 copy-start
  25.8 1.4 %copy.11 = bf16[1,128,128]{2,1,0:T(8,128)(2,1)} copy(bf16[1,128,128]{2,1,0:T(8,128)(2,1)} %get-tuple-element.4) | data formatting | bytes 65536
  27.2 0.0 copy-done
  27.2 0.6 %copy.12 = f32[2,32,128]{2,1,0:T(8,128)} copy(f32[2,32,128]{2,1,0:T(8,128)S(1)} %copy-done) | data formatting | bytes 65536
Async XLA Ops:
  25.8 1.4 %copy-start = (f32[2,32,128]{2,1,0:T(8,128)S(1)}, f32[2,32,128]{2,1,0:T(8,128)}, u32[]{:S(2)}) copy-start(f32[2,32,128]{2,1,0:T(8,128)} %get-tuple-element.5) | copy-start | bytes 98308

commit v4 on v3

--- a/solution.py
+++ b/solution.py
@@ -129,14 +129,14 @@
         ).wait_recv()
 
     loop(1, n, lambda d: table_copy(d).start())
-    own_feats(xf_send.at[0], across).start()
-    own_grad(xg_send.at[0], across).start()
 
     def send_column(d):
         own_feats(zf_send.at[d], column_target(d)).start()
         own_grad(zg_send.at[d], column_target(d)).start()
 
     loop(1, columns, lambda d: send_column(d))
+    own_feats(xf_send.at[0], across).start()
+    own_grad(xg_send.at[0], across).start()
 
     def arrive_column(d):
         block = column(d) + x

time: 28.1 us -> 28.1 us (level)
  no operation moved by 1% of the time
where the time goes in v4:
time: 28.1 us; the launch traced here: 27.8 us
  Pallas kernels  24.5 us (87%)
  local copies, waits for them, and re-layouts  2 us (7%)
  between operations  1.29 us (5%)
    pallas_call x1, Pallas kernels, local(): pl.pallas_call(functools.partial(kernel, n), out_shape=(jax.ShapeDtypeStr...  24.5 us
    unnamed x4, local copies, waits for them, and re-layouts  2 us

profile of v4, /device:TPU:0, one launch (start us, length us, event | category | flops | bytes accessed | tf_op | source)
XLA Modules:
  0.0 27.8 jit_solution(14198353884608854932)
XLA Ops:
  1.3 24.5 %backward.1 = (bf16[1,128,128]{2,1,0:T(8,128)(2,1)}, f32[2,32,128]{2,1,0:T(8,128)}) custom-call(bf16[1,128,256]{2,1,0:T(8,128)(2,1)} %feats.1, bf16[1,128,128]{2,1,0:T(8,128)(2,1)} %grad.1, bf16[256,128]{1,0:T(8,128)(2,1)} %w_qk_in.1, bf16[256,128]{1,0:T(8,128)(2,1)} %w_v_in.1, s32[1,2,4]{2,1,0:T(2,128)} %bitcast.1, s32[1]{0:T(128)S(6)} %copy.10.counts), custom_call_target="tpu_custom_call" | custom-call | tf_op jit(solution)/shard_map/backward/pallas_call | solution.py:272
  25.8 0.0 copy-start
  25.8 1.4 %copy.11 = bf16[1,128,128]{2,1,0:T(8,128)(2,1)} copy(bf16[1,128,128]{2,1,0:T(8,128)(2,1)} %get-tuple-element.4) | data formatting | bytes 65536
  27.2 0.0 copy-done
  27.2 0.6 %copy.12 = f32[2,32,128]{2,1,0:T(8,128)} copy(f32[2,32,128]{2,1,0:T(8,128)S(1)} %copy-done) | data formatting | bytes 65536
Async XLA Ops:
  25.8 1.4 %copy-start = (f32[2,32,128]{2,1,0:T(8,128)S(1)}, f32[2,32,128]{2,1,0:T(8,128)}, u32[]{:S(2)}) copy-start(f32[2,32,128]{2,1,0:T(8,128)} %get-tuple-element.5) | copy-start | bytes 98308
